TPU v7x, 32 devices: a whole 2x2x4 slice. The times are simulated.
32 devices in a mesh: row: 8 (over z, y), col: 4 (over x, core).
Axes of the slice: x: 2, y: 2, z: 4, core: 2. Of those that a mesh axis runs over, the one named last changes fastest.
Arguments:
- front: bfloat16 [8192, 8192], P('row', 'col'), may hold values from -0.125 to 0.125
- tile_mask: int32 [32, 32], P('row', 'col'), may hold values 0 or 1
- probes: bfloat16 [8192, 256], P(('col', 'row')), may hold values from -6 to 6
- coupling: float32 [8192, 256], P(('row', 'col')), may hold values from -0.375 to 0.375
Outputs:
- leaf_basis: float32 [8192, 256], P(('row', 'col'))
- upper_transfer: float32 [4, 8192, 256], P(None, ('row', 'col'))
Inputs may be any that keep to these rules, and one draw needn't show every extreme that they name: `tile_mask`: 1 where a tile of the front is present, 0 where it is absent.
All inputs are finite; a program needn't handle non-finite values. No bound on the sum of `tile_mask` on one device may be relied on, other than what follows from the above.
Results may differ from a plain program's by a relative error of at most 0.0003.
Values may be sent and summed in bfloat16 or wider, within the bound.
No kernel may reach another device: no remote copies, remote signals or barrier semaphores. Data moves between devices by JAX's collectives and lax.ppermute only.
A program may use at most 128 MiB of HBM per device.

v0:
```python
import jax
import jax.numpy as jnp
from jax import lax
from jax.sharding import PartitionSpec as P


def from_root(x, axis, root):
    mine = lax.axis_index(axis) == root
    return lax.psum(jnp.where(mine, x, jnp.zeros_like(x)), axis)


def from_partner(value, axis, distance):
    mask = 2**distance
    pairs = [(source, source ^ mask) for source in range(lax.axis_size(axis))]
    return lax.ppermute(value, axis, pairs)


def matmul_high(left, right):
    return jnp.matmul(left, right, precision=lax.Precision.HIGHEST)


def transpose_last(array):
    return jnp.swapaxes(array, -1, -2)


def merge_pair(top_node, bottom_node, level_index):
    top_s, top_w, top_p = top_node
    bottom_s, bottom_w, bottom_p = bottom_node
    if level_index > 1:
        factor = 2.0 ** (-(level_index - 1) / 2.0)
        top_s = top_s - factor * matmul_high(top_p, bottom_w)
        bottom_s = bottom_s - factor * matmul_high(bottom_p, top_w)
    stacked = jnp.concatenate([top_s, bottom_s], axis=-2)
    gram_matrix = matmul_high(transpose_last(stacked), stacked)
    probe_count = gram_matrix.shape[-1]
    shift_value = 0.001 * (jnp.trace(gram_matrix, axis1=-2, axis2=-1) / probe_count + 1e-06)
    gram_matrix = gram_matrix + shift_value[..., None, None] * jnp.eye(
        probe_count, dtype=jnp.float32
    )
    lower_factor = jnp.linalg.cholesky(gram_matrix)
    basis_rows = jax.scipy.linalg.solve_triangular(
        lower_factor, transpose_last(stacked), lower=True
    )
    new_w = matmul_high(basis_rows, jnp.concatenate([top_w, bottom_w], axis=-2))
    row_total = top_s.shape[-2]
    top_half = transpose_last(basis_rows[..., :row_total])
    bottom_half = transpose_last(basis_rows[..., row_total:])
    return ((transpose_last(lower_factor), new_w, top_p + bottom_p), top_half, bottom_half)


def pair_step(node_state, partner, side_bit, level_index):
    is_top = side_bit == 0
    top_node = tuple((jnp.where(is_top, mine, other) for mine, other in zip(node_state, partner)))
    bottom_node = tuple(
        (jnp.where(is_top, other, mine) for mine, other in zip(node_state, partner))
    )
    parent, top_half, bottom_half = merge_pair(top_node, bottom_node, level_index)
    return (parent, jnp.where(is_top, top_half, bottom_half))


def pack_state(node_state):
    return jnp.concatenate(node_state, axis=0)


def unpack_state(packed, sample_rows, probe_rows):
    return (
        packed[:sample_rows],
        packed[sample_rows : sample_rows + probe_rows],
        packed[sample_rows + probe_rows :],
    )


def shards(front, tile_mask, probes, coupling):
    col_count = lax.axis_size("col")
    row_count = lax.axis_size("row")
    row_index = lax.axis_index("row")
    col_index = lax.axis_index("col")
    leaf_rows = front.shape[0] // col_count
    probe_count = probes.shape[1]
    col_levels = col_count.bit_length() - 1
    row_levels = row_count.bit_length() - 1
    probe_block = lax.all_gather(probes, "row", axis=0, tiled=True)
    tile_above = row_index * col_count + jnp.arange(col_count, dtype=jnp.int32)
    tile_across = col_index * row_count + jnp.arange(row_count, dtype=jnp.int32)
    keep_tiles = tile_mask * (tile_above[:, None] // 2 != tile_across[None, :] // 2).astype(
        jnp.int32
    )
    masked = (
        front.reshape(col_count, leaf_rows, row_count, leaf_rows)
        * keep_tiles.astype(jnp.bfloat16)[:, None, :, None]
    )
    partial_value = jnp.dot(
        masked.reshape(front.shape), probe_block, preferred_element_type=jnp.float32
    )
    sample = lax.psum_scatter(partial_value, "col", scatter_dimension=0, tiled=True)
    offset = row_index * col_count % row_count * leaf_rows
    root_col = row_index * col_count // row_count
    offered = lax.dynamic_slice_in_dim(probe_block, offset, col_count * leaf_rows, 0)
    group_probes = from_root(offered, "col", root_col)
    own_probe = lax.dynamic_slice_in_dim(group_probes, col_index * leaf_rows, leaf_rows, 0).astype(
        jnp.float32
    )
    halves = []
    node_state = (sample, own_probe, coupling)
    for bit_index in range(col_levels):
        sample_rows = node_state[0].shape[0]
        probe_rows = node_state[1].shape[0]
        packed = from_partner(pack_state(node_state), "col", bit_index)
        partner = unpack_state(packed, sample_rows, probe_rows)
        node_state, own_half = pair_step(
            node_state, partner, col_index >> bit_index & 1, bit_index + 1
        )
        halves.append(own_half)
    for bit_index in range(row_levels):
        packed = from_partner(pack_state(node_state), "row", bit_index)
        partner = unpack_state(packed, probe_count, probe_count)
        node_state, own_half = pair_step(
            node_state, partner, row_index >> bit_index & 1, col_levels + bit_index + 1
        )
        halves.append(own_half)
    return (halves[0], jnp.stack(halves[1:], axis=0))


def solution(mesh):
    in_specs = (P("row", "col"), P("row", "col"), P(("col", "row"), None), P(("row", "col"), None))
    out_specs = (P(("row", "col"), None), P(None, ("row", "col"), None))
    return jax.shard_map(shards, mesh=mesh, in_specs=in_specs, out_specs=out_specs, check_vma=False)
```

profile of v0, /device:TPU:0, one launch (start us, length us, event | category | flops | bytes accessed | tf_op | source)
XLA Modules:
  0.0 565.7 jit_solution(5704452580519430025)
XLA Ops:
  7.2 1.7 copy.6
  10.1 3.4 copy.83
  13.5 39.2 %all-gather.2.cloned.1.call-done = bf16[2048,256]{0,1:T(8,128)(2,1)} async-done(((bf16[256,256]{0,1:T(8,128)(2,1)}), bf16[2048,256]{0,1:T(8,128)(2,1)}) %all-gather.2.cloned.1.call-update) | async-done | bytes 1048592 | tf_op jit(solution)/shard_map/all_gather | solution.py:82
  52.7 2.0 dynamic-slice_select_fusion
  55.0 6.0 %fusion = f32[1024,256]{0,1:T(8,128)} fusion(bf16[2048,256]{0,1:T(8,128)(2,1)} %all-gather.2.cloned.1.call-done, bf16[1024,2048]{1,0:T(8,128)(2,1)} %param.7, bf16[1024,2048]{1,0:T(8,128)(2,1)} %bitcast.194), kind=kOutput, calls=%fused_computation.10 | convolution fusion | flops 1075838976 | bytes 10485760 | tf_op jit(solution)/shard_map/dot_general | solution.py:92
  61.1 26.4 %all-reduce.3.cloned.1.call-done = bf16[1024,256]{0,1:T(8,128)(2,1)} async-done(((bf16[1024,256]{0,1:T(8,128)(2,1)}), bf16[1024,256]{0,1:T(8,128)(2,1)}) %all-reduce.3.cloned.1.call-update) | async-done | bytes 524304 | tf_op jit(solution)/shard_map/psum | solution.py:9
  88.4 27.1 %reduce-scatter.2.cloned.1.call-done = f32[256,256]{0,1:T(8,128)} async-done(((f32[1024,256]{0,1:T(8,128)}), f32[256,256]{0,1:T(8,128)}) %reduce-scatter.2.cloned.1.call-update) | async-done | bytes 262160 | tf_op jit(solution)/shard_map/reduce_scatter | solution.py:95
  116.6 2.3 collective-permute-done
  122.1 11.7 %cholesky.256 = f32[128,128]{1,0:T(8,128)S(1)} custom-call(f32[128,128]{1,0:T(8,128)S(1)} %cholesky.422), custom_call_target="Cholesky" | custom-call | tf_op jit(solution)/shard_map/jit(cholesky)/cholesky | solution.py:40
  133.9 9.8 %custom-call.19 = f32[1,128,128]{1,2,0:T(8,128)S(1)} custom-call(f32[1,128,128]{2,1,0:T(8,128)S(1)} %get-tuple-element.134), custom_call_target="InvertDiagBlocksLowerTriangular" | custom-call | tf_op jit(solution)/shard_map/jit(cholesky)/cholesky | solution.py:40
  144.5 12.1 %cholesky.273 = f32[128,128]{1,0:T(8,128)S(1)} custom-call(f32[128,128]{1,0:T(8,128)S(1)} %convolution_subtract_fusion.9), custom_call_target="Cholesky" | custom-call | tf_op jit(solution)/shard_map/jit(cholesky)/cholesky | solution.py:40
  158.8 4.1 while.10
  162.9 19.7 %custom-call.20 = f32[2,128,128]{1,2,0:T(8,128)S(1)} custom-call(f32[2,128,128]{2,1,0:T(8,128)S(1)} %get-tuple-element.36), custom_call_target="InvertDiagBlocksLowerTriangular" | custom-call | tf_op jit(solution)/shard_map/jit(_solve_triangular)/triangular_solve | solution.py:41
  185.3 19.2 %collective-permute-done.1 = f32[768,256]{0,1:T(8,128)S(1)} collective-permute-done((f32[768,256]{0,1:T(8,128)S(1)}, f32[768,256]{0,1:T(8,128)S(1)}, u32[]{:S(2)}, u32[]{:S(2)}) %collective-permute-start.1) | collective-permute-done | bytes 786464 | tf_op jit(solution)/shard_map/ppermute | solution.py:15
  207.6 11.7 %cholesky.290 = f32[128,128]{1,0:T(8,128)S(1)} custom-call(f32[128,128]{1,0:T(8,128)S(1)} %cholesky.425), custom_call_target="Cholesky" | custom-call | tf_op jit(solution)/shard_map/jit(cholesky)/cholesky | solution.py:40
  219.4 9.8 %custom-call.21 = f32[1,128,128]{1,2,0:T(8,128)S(1)} custom-call(f32[1,128,128]{2,1,0:T(8,128)S(1)} %get-tuple-element.130), custom_call_target="InvertDiagBlocksLowerTriangular" | custom-call | tf_op jit(solution)/shard_map/jit(cholesky)/cholesky | solution.py:40
  229.9 11.9 %cholesky.307 = f32[128,128]{1,0:T(8,128)S(1)} custom-call(f32[128,128]{1,0:T(8,128)S(1)} %convolution_subtract_fusion.8), custom_call_target="Cholesky" | custom-call | tf_op jit(solution)/shard_map/jit(cholesky)/cholesky | solution.py:40
  244.5 4.0 while.11
  248.5 19.7 %custom-call.22 = f32[2,128,128]{1,2,0:T(8,128)S(1)} custom-call(f32[2,128,128]{2,1,0:T(8,128)S(1)} %get-tuple-element.37), custom_call_target="InvertDiagBlocksLowerTriangular" | custom-call | tf_op jit(solution)/shard_map/jit(_solve_triangular)/triangular_solve | solution.py:41
  270.4 1.5 collective-permute-start.2
  271.9 17.4 %collective-permute-done.2 = f32[768,256]{0,1:T(8,128)} collective-permute-done((f32[768,256]{0,1:T(8,128)S(1)}, f32[768,256]{0,1:T(8,128)}, u32[]{:S(2)}, u32[]{:S(2)}) %collective-permute-start.2) | collective-permute-done | bytes 786464 | tf_op jit(solution)/shard_map/ppermute | solution.py:15
  290.4 1.4 select_subtract_fusion.5
  291.9 1.4 select_subtract_fusion.4
  295.5 11.7 %cholesky.324 = f32[128,128]{1,0:T(8,128)S(1)} custom-call(f32[128,128]{1,0:T(8,128)S(1)} %cholesky.428), custom_call_target="Cholesky" | custom-call | tf_op jit(solution)/shard_map/jit(cholesky)/cholesky | solution.py:40
  307.2 9.8 %custom-call.23 = f32[1,128,128]{1,2,0:T(8,128)S(1)} custom-call(f32[1,128,128]{2,1,0:T(8,128)S(1)} %get-tuple-element.126), custom_call_target="InvertDiagBlocksLowerTriangular" | custom-call | tf_op jit(solution)/shard_map/jit(cholesky)/cholesky | solution.py:40
  317.7 12.1 %cholesky.341 = f32[128,128]{1,0:T(8,128)S(1)} custom-call(f32[128,128]{1,0:T(8,128)S(1)} %convolution_subtract_fusion.7), custom_call_target="Cholesky" | custom-call | tf_op jit(solution)/shard_map/jit(cholesky)/cholesky | solution.py:40
  332.5 4.0 while.12
  336.5 19.7 %custom-call.24 = f32[2,128,128]{1,2,0:T(8,128)S(1)} custom-call(f32[2,128,128]{2,1,0:T(8,128)S(1)} %get-tuple-element.38), custom_call_target="InvertDiagBlocksLowerTriangular" | custom-call | tf_op jit(solution)/shard_map/jit(_solve_triangular)/triangular_solve | solution.py:41
  358.5 1.5 collective-permute-start.3
  360.0 16.5 %collective-permute-done.3 = f32[768,256]{0,1:T(8,128)} collective-permute-done((f32[768,256]{0,1:T(8,128)S(1)}, f32[768,256]{0,1:T(8,128)}, u32[]{:S(2)}, u32[]{:S(2)}) %collective-permute-start.3) | collective-permute-done | bytes 786464 | tf_op jit(solution)/shard_map/ppermute | solution.py:15
  377.6 1.4 select_subtract_fusion.3
  379.1 1.4 select_subtract_fusion.2
  384.3 11.7 %cholesky.358 = f32[128,128]{1,0:T(8,128)S(1)} custom-call(f32[128,128]{1,0:T(8,128)S(1)} %cholesky.431), custom_call_target="Cholesky" | custom-call | tf_op jit(solution)/shard_map/jit(cholesky)/cholesky | solution.py:40
  396.1 9.8 %custom-call.25 = f32[1,128,128]{1,2,0:T(8,128)S(1)} custom-call(f32[1,128,128]{2,1,0:T(8,128)S(1)} %get-tuple-element.122), custom_call_target="InvertDiagBlocksLowerTriangular" | custom-call | tf_op jit(solution)/shard_map/jit(cholesky)/cholesky | solution.py:40
  408.3 11.9 %cholesky.375 = f32[128,128]{1,0:T(8,128)S(1)} custom-call(f32[128,128]{1,0:T(8,128)S(1)} %convolution_subtract_fusion.6), custom_call_target="Cholesky" | custom-call | tf_op jit(solution)/shard_map/jit(cholesky)/cholesky | solution.py:40
  423.9 4.0 while.13
  429.3 20.5 %custom-call.26 = f32[2,128,128]{1,2,0:T(8,128)S(1)} custom-call(f32[2,128,128]{2,1,0:T(8,128)} %copy-done.7), custom_call_target="InvertDiagBlocksLowerTriangular" | custom-call | tf_op jit(solution)/shard_map/jit(_solve_triangular)/triangular_solve | solution.py:41
  450.2 1.9 convolution_subtract_fusion.1
  452.3 1.5 fusion.97
  455.4 2.4 collective-permute-start.4
  460.7 29.8 %collective-permute-done.4 = f32[768,256]{0,1:T(8,128)} collective-permute-done((f32[768,256]{0,1:T(8,128)}, f32[768,256]{0,1:T(8,128)}, u32[]{:S(2)}, u32[]{:S(2)}) %collective-permute-start.4) | collective-permute-done | bytes 786464 | tf_op jit(solution)/shard_map/ppermute | solution.py:15
  490.5 1.5 select_subtract_fusion.1
  492.0 1.5 select_subtract_fusion
  495.8 11.7 %cholesky.392 = f32[128,128]{1,0:T(8,128)S(1)} custom-call(f32[128,128]{1,0:T(8,128)S(1)} %cholesky.434), custom_call_target="Cholesky" | custom-call | tf_op jit(solution)/shard_map/jit(cholesky)/cholesky | solution.py:40
  507.6 9.8 %custom-call.27 = f32[1,128,128]{1,2,0:T(8,128)S(1)} custom-call(f32[1,128,128]{2,1,0:T(8,128)S(1)} %get-tuple-element.118), custom_call_target="InvertDiagBlocksLowerTriangular" | custom-call | tf_op jit(solution)/shard_map/jit(cholesky)/cholesky | solution.py:40
  517.9 11.9 %cholesky.409 = f32[128,128]{1,0:T(8,128)S(1)} custom-call(f32[128,128]{1,0:T(8,128)S(1)} %convolution_subtract_fusion.5), custom_call_target="Cholesky" | custom-call | tf_op jit(solution)/shard_map/jit(cholesky)/cholesky | solution.py:40
  532.5 4.1 while.14
  536.7 19.7 %custom-call.28 = f32[2,128,128]{1,2,0:T(8,128)S(1)} custom-call(f32[2,128,128]{2,1,0:T(8,128)S(1)} %get-tuple-element.40), custom_call_target="InvertDiagBlocksLowerTriangular" | custom-call | tf_op jit(solution)/shard_map/jit(_solve_triangular)/triangular_solve | solution.py:41
  (183 shorter events, 65.3 us)
Async XLA Ops:
  7.2 45.6 %all-gather.2.cloned.1.call-start = ((), (), s32[]{:S(2)}) async-start(), calls=%async_computation.1 | async-start | bytes 1179648 | tf_op jit(solution)/shard_map/all_gather | solution.py:82
  8.9 78.6 %all-reduce.3.cloned.1.call-start = ((), (), s32[]{:S(2)}) async-start(), calls=%async_computation.3 | async-start | bytes 1048576 | tf_op jit(solution)/shard_map/psum | solution.py:9
  54.7 60.8 %reduce-scatter.2.cloned.1.call-start = ((), (), s32[]{:S(2)}) async-start(), calls=%async_computation.2 | async-start | bytes 1310720 | tf_op jit(solution)/shard_map/reduce_scatter | solution.py:95
  55.0 6.0 %copy-start.6 = (f32[256,256]{1,0:T(8,128)S(1)}, f32[256,256]{1,0:T(8,128)}, u32[]{:S(2)}) copy-start(f32[256,256]{1,0:T(8,128)} %param.10) | copy-start | bytes 786436
  116.5 2.4 collective-permute-start
  184.8 19.7 %collective-permute-start.1 = (f32[768,256]{0,1:T(8,128)S(1)}, f32[768,256]{0,1:T(8,128)S(1)}, u32[]{:S(2)}, u32[]{:S(2)}) collective-permute-start(f32[768,256]{0,1:T(8,128)S(1)} %pad_maximum_fusion.2), channel_id=1, source_target_pairs={{0,2},{1,3},{2,0},{3,1},{4,6},{5,7},{6,4},{7,5},{8,10},{9,11},{10,... | collective-permute-start | bytes 2359304 | tf_op jit(solution)/shard_map/ppermute | solution.py:15
  270.4 18.9 %collective-permute-start.2 = (f32[768,256]{0,1:T(8,128)S(1)}, f32[768,256]{0,1:T(8,128)}, u32[]{:S(2)}, u32[]{:S(2)}) collective-permute-start(f32[768,256]{0,1:T(8,128)S(1)} %pad_maximum_fusion.3), channel_id=1, source_target_pairs={{0,4},{4,0},{8,12},{12,8},{16,20},{20,16},{24,28},{28,24},{1,5},{5... | collective-permute-start | bytes 2359304 | tf_op jit(solution)/shard_map/ppermute | solution.py:15
  358.5 18.0 %collective-permute-start.3 = (f32[768,256]{0,1:T(8,128)S(1)}, f32[768,256]{0,1:T(8,128)}, u32[]{:S(2)}, u32[]{:S(2)}) collective-permute-start(f32[768,256]{0,1:T(8,128)S(1)} %pad_maximum_fusion.4), channel_id=1, source_target_pairs={{0,8},{4,12},{8,0},{12,4},{16,24},{20,28},{24,16},{28,20},{1,9},{5... | collective-permute-start | bytes 2359304 | tf_op jit(solution)/shard_map/ppermute | solution.py:15
  384.3 11.8 %copy-start.5 = (f32[256,256]{1,0:T(8,128)}, f32[256,256]{1,0:T(8,128)S(1)}, u32[]{:S(2)}) copy-start(f32[256,256]{1,0:T(8,128)S(1)} %fusion.58) | copy-start | bytes 786436
  420.2 2.7 copy-start.1
  427.9 0.7 copy-start.7
  428.6 0.7 copy-start
  455.4 35.1 %collective-permute-start.4 = (f32[768,256]{0,1:T(8,128)}, f32[768,256]{0,1:T(8,128)}, u32[]{:S(2)}, u32[]{:S(2)}) collective-permute-start(f32[768,256]{0,1:T(8,128)} %pad_maximum_fusion.5), channel_id=1, source_target_pairs={{0,16},{4,20},{8,24},{12,28},{16,0},{20,4},{24,8},{28,12},{1,17},{... | collective-permute-start | bytes 2359304 | tf_op jit(solution)/shard_map/ppermute | solution.py:15
  494.8 63.1 %copy-start.2 = (f32[1,256,256]{2,1,0:T(8,128)S(1)}, f32[1,256,256]{2,1,0:T(8,128)}, u32[]{:S(2)}) copy-start(f32[1,256,256]{2,1,0:T(8,128)} %fusion.41) | copy-start | bytes 786436
  494.8 63.1 %copy-start.3 = (f32[1,256,256]{2,1,0:T(8,128)S(1)}, f32[1,256,256]{2,1,0:T(8,128)}, u32[]{:S(2)}) copy-start(f32[1,256,256]{2,1,0:T(8,128)} %fusion.37) | copy-start | bytes 786436
  494.8 63.1 %copy-start.4 = (f32[1,256,256]{2,1,0:T(8,128)S(1)}, f32[1,256,256]{2,1,0:T(8,128)}, u32[]{:S(2)}) copy-start(f32[1,256,256]{2,1,0:T(8,128)} %fusion.33) | copy-start | bytes 786436
Sparse Core Ops, SparseCore 0:
  10.6 42.1 all-gather.1
  55.1 32.3 all-reduce.2
  90.6 24.8 reduce-scatter.1
where the time goes:
time: 569 us; the launch traced here: 566 us
  other arithmetic  289 us (51%)
  waiting for transfers between devices  178 us (31%)
  matrix products  38.1 us (7%)
  local copies, waits for them, and re-layouts  29.5 us (5%)
  between operations  25 us (4%)
  starting transfers between devices  6.23 us (1%)
    another operation x34, other arithmetic, merge_pair(): lower_factor = jnp.linalg.cholesky(gram_matrix)  174 us
    another operation x10, other arithmetic, merge_pair(): jax.scipy.linalg.solve_triangular(lower_factor, transpose_last(stacked),...  100 us
    ppermute x5, waiting for transfers between devices, from_partner(): return lax.ppermute(value, axis, pairs)  85.1 us
    all_gather x1, waiting for transfers between devices, shards(): probe_block = lax.all_gather(probes, 'row', axis=0, tiled=True)  39.2 us
    reduce_scatter x1, waiting for transfers between devices, shards(): lax.psum_scatter(partial_value, 'col', scatter_dimension=0, tiled=True)  27.1 us
    psum x1, waiting for transfers between devices, from_root(): return lax.psum(jnp.where(mine, x, jnp.zeros_like(x)), axis)  26.4 us
    another operation x41, local copies, waits for them, and re-layouts, merge_pair(): jax.scipy.linalg.solve_triangular(lower_factor, transpose_last(stacked),...  20.7 us
    dot_general x17, matrix products, matmul_high(): return jnp.matmul(left, right, precision=lax.Precision.HIGHEST)  18.2 us
  transfers between devices with their start and end apart: 8, of which 8 were waited for; matrix products, arithmetic and copies ran while one was open for 3% of the time, Pallas kernels for 0%

commit v1 on v0

--- a/solution.py
+++ b/solution.py
@@ -79,7 +79,14 @@
     probe_count = probes.shape[1]
     col_levels = col_count.bit_length() - 1
     row_levels = row_count.bit_length() - 1
-    probe_block = lax.all_gather(probes, "row", axis=0, tiled=True)
+    ways = lax.axis_size("row")
+    pieces = [probes]
+    for far in range(1, ways):
+        pieces.append(
+            lax.ppermute(pieces[far - 1], "row", [(d, (d - 1) % ways) for d in range(ways)])
+        )
+    line = jnp.concatenate(pieces, axis=0)
+    probe_block = jnp.roll(line, lax.axis_index("row") * probes.shape[0], axis=0)
     tile_above = row_index * col_count + jnp.arange(col_count, dtype=jnp.int32)
     tile_across = col_index * row_count + jnp.arange(row_count, dtype=jnp.int32)
     keep_tiles = tile_mask * (tile_above[:, None] // 2 != tile_across[None, :] // 2).astype(

time: 569 us -> 584 us (1.026)
  starting transfers between devices: 6.23 us -> 41.3 us
  waiting for transfers between devices: 178 us -> 158 us
    all_gather x1 -> x0, waiting for transfers between devices: 39.2 us -> none  [shards(): probe_block = lax.all_gather(probes, 'row', axis=0, tiled=True)]
    ppermute x0 -> x7, starting transfers between devices: none -> 35 us  [shards(): lax.ppermute(pieces[far - 1], 'row', [(d, (d - 1) % ways) for d in range(...]
    ppermute x0 -> x7, waiting for transfers between devices: none -> 16.8 us  [shards(): lax.ppermute(pieces[far - 1], 'row', [(d, (d - 1) % ways) for d in range(...]
  transfers between devices with their start and end apart: 8 -> 14, of which waited for: 8 -> 13; matrix products, arithmetic and copies ran while one was open for 3% -> 2% of each run, Pallas kernels for 0% -> 0%
where the time goes in v1:
time: 584 us; the launch traced here: 580 us
  other arithmetic  288 us (49%)
  waiting for transfers between devices  158 us (27%)
  starting transfers between devices  41.3 us (7%)
  matrix products  37.9 us (6%)
  local copies, waits for them, and re-layouts  29 us (5%)
  between operations  25.3 us (4%)
    another operation x34, other arithmetic, merge_pair(): lower_factor = jnp.linalg.cholesky(gram_matrix)  174 us
    another operation x10, other arithmetic, merge_pair(): jax.scipy.linalg.solve_triangular(lower_factor, transpose_last(stacked),...  100 us
    ppermute x5, waiting for transfers between devices, from_partner(): return lax.ppermute(value, axis, pairs)  85 us
    ppermute x7, starting transfers between devices, shards(): lax.ppermute(pieces[far - 1], 'row', [(d, (d - 1) % ways) for d in range(...  35 us
    psum x1, waiting for transfers between devices, from_root(): return lax.psum(jnp.where(mine, x, jnp.zeros_like(x)), axis)  29.2 us
    reduce_scatter x1, waiting for transfers between devices, shards(): lax.psum_scatter(partial_value, 'col', scatter_dimension=0, tiled=True)  27.1 us
    another operation x41, local copies, waits for them, and re-layouts, merge_pair(): jax.scipy.linalg.solve_triangular(lower_factor, transpose_last(stacked),...  20.7 us
    dot_general x17, matrix products, matmul_high(): return jnp.matmul(left, right, precision=lax.Precision.HIGHEST)  18.2 us
  transfers between devices with their start and end apart: 14, of which 13 were waited for; matrix products, arithmetic and copies ran while one was open for 2% of the time, Pallas kernels for 0%

profile of v1, /device:TPU:0, one launch (start us, length us, event | category | flops | bytes accessed | tf_op | source)
XLA Modules:
  0.0 579.9 jit_solution(11873710764518402263)
XLA Ops:
  8.2 6.1 %collective-permute-start = (bf16[256,256]{0,1:T(8,128)(2,1)S(1)}, bf16[256,256]{0,1:T(8,128)(2,1)S(1)}, u32[]{:S(2)}, u32[]{:S(2)}) collective-permute-start(bf16[256,256]{0,1:T(8,128)(2,1)S(1)} %copy.7), channel_id=1, source_target_pairs={{0,28},{4,0},{8,4},{12,8},{16,12},{20,16},{24,20},{28,24},{1,29},{... | collective-permute-start | bytes 393224 | tf_op jit(solution)/shard_map/ppermute | solution.py:86
  14.3 2.8 collective-permute-done
  17.1 5.2 collective-permute-start.1
  22.2 2.5 collective-permute-done.1
  24.8 5.1 collective-permute-start.2
  29.9 2.5 collective-permute-done.2
  32.4 5.1 collective-permute-start.3
  38.7 3.4 copy.85
  42.1 3.1 collective-permute-start.4
  45.3 2.8 collective-permute-done.4
  48.0 5.2 collective-permute-start.5
  53.3 3.8 collective-permute-done.5
  57.0 5.2 collective-permute-start.6
  62.3 2.5 collective-permute-done.6
  66.3 5.8 fusion
  72.2 29.2 %all-reduce.3.cloned.1.call-done = bf16[1024,256]{0,1:T(8,128)(2,1)} async-done(((bf16[1024,256]{0,1:T(8,128)(2,1)}), bf16[1024,256]{0,1:T(8,128)(2,1)}) %all-reduce.3.cloned.1.call-update) | async-done | bytes 524304 | tf_op jit(solution)/shard_map/psum | solution.py:9
  102.4 27.1 %reduce-scatter.2.cloned.1.call-done = f32[256,256]{0,1:T(8,128)} async-done(((f32[1024,256]{0,1:T(8,128)}), f32[256,256]{0,1:T(8,128)}) %reduce-scatter.2.cloned.1.call-update) | async-done | bytes 262160 | tf_op jit(solution)/shard_map/reduce_scatter | solution.py:102
  130.6 2.3 collective-permute-done.7
  136.1 11.7 %cholesky.256 = f32[128,128]{1,0:T(8,128)S(1)} custom-call(f32[128,128]{1,0:T(8,128)S(1)} %cholesky.422), custom_call_target="Cholesky" | custom-call | tf_op jit(solution)/shard_map/jit(cholesky)/cholesky | solution.py:40
  147.8 9.8 %custom-call.19 = f32[1,128,128]{1,2,0:T(8,128)S(1)} custom-call(f32[1,128,128]{2,1,0:T(8,128)S(1)} %get-tuple-element.134), custom_call_target="InvertDiagBlocksLowerTriangular" | custom-call | tf_op jit(solution)/shard_map/jit(cholesky)/cholesky | solution.py:40
  158.4 12.1 %cholesky.273 = f32[128,128]{1,0:T(8,128)S(1)} custom-call(f32[128,128]{1,0:T(8,128)S(1)} %convolution_subtract_fusion.9), custom_call_target="Cholesky" | custom-call | tf_op jit(solution)/shard_map/jit(cholesky)/cholesky | solution.py:40
  172.8 4.1 while.10
  176.9 19.7 %custom-call.20 = f32[2,128,128]{1,2,0:T(8,128)S(1)} custom-call(f32[2,128,128]{2,1,0:T(8,128)S(1)} %get-tuple-element.36), custom_call_target="InvertDiagBlocksLowerTriangular" | custom-call | tf_op jit(solution)/shard_map/jit(_solve_triangular)/triangular_solve | solution.py:41
  199.2 19.2 %collective-permute-done.8 = f32[768,256]{0,1:T(8,128)S(1)} collective-permute-done((f32[768,256]{0,1:T(8,128)S(1)}, f32[768,256]{0,1:T(8,128)S(1)}, u32[]{:S(2)}, u32[]{:S(2)}) %collective-permute-start.8) | collective-permute-done | bytes 786464 | tf_op jit(solution)/shard_map/ppermute | solution.py:15
  221.6 11.7 %cholesky.290 = f32[128,128]{1,0:T(8,128)S(1)} custom-call(f32[128,128]{1,0:T(8,128)S(1)} %cholesky.425), custom_call_target="Cholesky" | custom-call | tf_op jit(solution)/shard_map/jit(cholesky)/cholesky | solution.py:40
  233.3 9.8 %custom-call.21 = f32[1,128,128]{1,2,0:T(8,128)S(1)} custom-call(f32[1,128,128]{2,1,0:T(8,128)S(1)} %get-tuple-element.130), custom_call_target="InvertDiagBlocksLowerTriangular" | custom-call | tf_op jit(solution)/shard_map/jit(cholesky)/cholesky | solution.py:40
  243.8 11.9 %cholesky.307 = f32[128,128]{1,0:T(8,128)S(1)} custom-call(f32[128,128]{1,0:T(8,128)S(1)} %convolution_subtract_fusion.8), custom_call_target="Cholesky" | custom-call | tf_op jit(solution)/shard_map/jit(cholesky)/cholesky | solution.py:40
  258.4 4.0 while.11
  262.4 19.7 %custom-call.22 = f32[2,128,128]{1,2,0:T(8,128)S(1)} custom-call(f32[2,128,128]{2,1,0:T(8,128)S(1)} %get-tuple-element.37), custom_call_target="InvertDiagBlocksLowerTriangular" | custom-call | tf_op jit(solution)/shard_map/jit(_solve_triangular)/triangular_solve | solution.py:41
  285.9 17.3 %collective-permute-done.9 = f32[768,256]{0,1:T(8,128)} collective-permute-done((f32[768,256]{0,1:T(8,128)S(1)}, f32[768,256]{0,1:T(8,128)}, u32[]{:S(2)}, u32[]{:S(2)}) %collective-permute-start.9) | collective-permute-done | bytes 786464 | tf_op jit(solution)/shard_map/ppermute | solution.py:15
  309.4 11.7 %cholesky.324 = f32[128,128]{1,0:T(8,128)S(1)} custom-call(f32[128,128]{1,0:T(8,128)S(1)} %cholesky.428), custom_call_target="Cholesky" | custom-call | tf_op jit(solution)/shard_map/jit(cholesky)/cholesky | solution.py:40
  321.1 9.8 %custom-call.23 = f32[1,128,128]{1,2,0:T(8,128)S(1)} custom-call(f32[1,128,128]{2,1,0:T(8,128)S(1)} %get-tuple-element.126), custom_call_target="InvertDiagBlocksLowerTriangular" | custom-call | tf_op jit(solution)/shard_map/jit(cholesky)/cholesky | solution.py:40
  331.7 12.1 %cholesky.341 = f32[128,128]{1,0:T(8,128)S(1)} custom-call(f32[128,128]{1,0:T(8,128)S(1)} %convolution_subtract_fusion.7), custom_call_target="Cholesky" | custom-call | tf_op jit(solution)/shard_map/jit(cholesky)/cholesky | solution.py:40
  346.5 4.0 while.12
  350.5 19.7 %custom-call.24 = f32[2,128,128]{1,2,0:T(8,128)S(1)} custom-call(f32[2,128,128]{2,1,0:T(8,128)S(1)} %get-tuple-element.38), custom_call_target="InvertDiagBlocksLowerTriangular" | custom-call | tf_op jit(solution)/shard_map/jit(_solve_triangular)/triangular_solve | solution.py:41
  373.9 16.5 %collective-permute-done.10 = f32[768,256]{0,1:T(8,128)} collective-permute-done((f32[768,256]{0,1:T(8,128)S(1)}, f32[768,256]{0,1:T(8,128)}, u32[]{:S(2)}, u32[]{:S(2)}) %collective-permute-start.10) | collective-permute-done | bytes 786464 | tf_op jit(solution)/shard_map/ppermute | solution.py:15
  398.3 11.7 %cholesky.358 = f32[128,128]{1,0:T(8,128)S(1)} custom-call(f32[128,128]{1,0:T(8,128)S(1)} %cholesky.431), custom_call_target="Cholesky" | custom-call | tf_op jit(solution)/shard_map/jit(cholesky)/cholesky | solution.py:40
  410.0 9.8 %custom-call.25 = f32[1,128,128]{1,2,0:T(8,128)S(1)} custom-call(f32[1,128,128]{2,1,0:T(8,128)S(1)} %get-tuple-element.122), custom_call_target="InvertDiagBlocksLowerTriangular" | custom-call | tf_op jit(solution)/shard_map/jit(cholesky)/cholesky | solution.py:40
  422.2 11.9 %cholesky.375 = f32[128,128]{1,0:T(8,128)S(1)} custom-call(f32[128,128]{1,0:T(8,128)S(1)} %convolution_subtract_fusion.6), custom_call_target="Cholesky" | custom-call | tf_op jit(solution)/shard_map/jit(cholesky)/cholesky | solution.py:40
  437.8 4.0 while.13
  443.2 20.5 %custom-call.26 = f32[2,128,128]{1,2,0:T(8,128)S(1)} custom-call(f32[2,128,128]{2,1,0:T(8,128)} %copy-done.7), custom_call_target="InvertDiagBlocksLowerTriangular" | custom-call | tf_op jit(solution)/shard_map/jit(_solve_triangular)/triangular_solve | solution.py:41
  469.3 2.4 collective-permute-start.11
  474.7 29.7 %collective-permute-done.11 = f32[768,256]{0,1:T(8,128)} collective-permute-done((f32[768,256]{0,1:T(8,128)}, f32[768,256]{0,1:T(8,128)}, u32[]{:S(2)}, u32[]{:S(2)}) %collective-permute-start.11) | collective-permute-done | bytes 786464 | tf_op jit(solution)/shard_map/ppermute | solution.py:15
  509.6 11.7 %cholesky.392 = f32[128,128]{1,0:T(8,128)S(1)} custom-call(f32[128,128]{1,0:T(8,128)S(1)} %cholesky.434), custom_call_target="Cholesky" | custom-call | tf_op jit(solution)/shard_map/jit(cholesky)/cholesky | solution.py:40
  521.4 9.8 %custom-call.27 = f32[1,128,128]{1,2,0:T(8,128)S(1)} custom-call(f32[1,128,128]{2,1,0:T(8,128)S(1)} %get-tuple-element.118), custom_call_target="InvertDiagBlocksLowerTriangular" | custom-call | tf_op jit(solution)/shard_map/jit(cholesky)/cholesky | solution.py:40
  531.7 11.9 %cholesky.409 = f32[128,128]{1,0:T(8,128)S(1)} custom-call(f32[128,128]{1,0:T(8,128)S(1)} %convolution_subtract_fusion.5), custom_call_target="Cholesky" | custom-call | tf_op jit(solution)/shard_map/jit(cholesky)/cholesky | solution.py:40
  546.4 4.1 while.14
  550.5 19.7 %custom-call.28 = f32[2,128,128]{1,2,0:T(8,128)S(1)} custom-call(f32[2,128,128]{2,1,0:T(8,128)S(1)} %get-tuple-element.40), custom_call_target="InvertDiagBlocksLowerTriangular" | custom-call | tf_op jit(solution)/shard_map/jit(_solve_triangular)/triangular_solve | solution.py:41
  (210 shorter events, 82.9 us)
Async XLA Ops:
  7.2 94.3 %all-reduce.3.cloned.1.call-start = ((), (), s32[]{:S(2)}) async-start(), calls=%async_computation.2 | async-start | bytes 1048576 | tf_op jit(solution)/shard_map/psum | solution.py:9
  8.2 8.8 %collective-permute-start = (bf16[256,256]{0,1:T(8,128)(2,1)S(1)}, bf16[256,256]{0,1:T(8,128)(2,1)S(1)}, u32[]{:S(2)}, u32[]{:S(2)}) collective-permute-start(bf16[256,256]{0,1:T(8,128)(2,1)S(1)} %copy.7), channel_id=1, source_target_pairs={{0,28},{4,0},{8,4},{12,8},{16,12},{20,16},{24,20},{28,24},{1,29},{... | collective-permute-start | bytes 393224 | tf_op jit(solution)/shard_map/ppermute | solution.py:86
  17.1 7.7 %collective-permute-start.1 = (bf16[256,256]{0,1:T(8,128)(2,1)S(1)}, bf16[256,256]{0,1:T(8,128)(2,1)S(1)}, u32[]{:S(2)}, u32[]{:S(2)}) collective-permute-start(bf16[256,256]{0,1:T(8,128)(2,1)S(1)} %collective-permute-done), channel_id=1, source_target_pairs={{0,28},{4,0},{8,4},{12,8},{16,12},{20,16},{24,20},{28,24},{1,29},{... | collective-permute-start | bytes 393224 | tf_op jit(solution)/shard_map/ppermute | solution.py:86
  24.8 7.7 %collective-permute-start.2 = (bf16[256,256]{0,1:T(8,128)(2,1)S(1)}, bf16[256,256]{0,1:T(8,128)(2,1)S(1)}, u32[]{:S(2)}, u32[]{:S(2)}) collective-permute-start(bf16[256,256]{0,1:T(8,128)(2,1)S(1)} %collective-permute-done.1), channel_id=1, source_target_pairs={{0,28},{4,0},{8,4},{12,8},{16,12},{20,16},{24,20},{28,24},{1,29},{... | collective-permute-start | bytes 393224 | tf_op jit(solution)/shard_map/ppermute | solution.py:86
  32.4 9.7 %collective-permute-start.3 = (bf16[256,256]{0,1:T(8,128)(2,1)S(1)}, bf16[256,256]{0,1:T(8,128)(2,1)S(1)}, u32[]{:S(2)}, u32[]{:S(2)}) collective-permute-start(bf16[256,256]{0,1:T(8,128)(2,1)S(1)} %collective-permute-done.2), channel_id=1, source_target_pairs={{0,28},{4,0},{8,4},{12,8},{16,12},{20,16},{24,20},{28,24},{1,29},{... | collective-permute-start | bytes 393224 | tf_op jit(solution)/shard_map/ppermute | solution.py:86
  42.1 6.0 %collective-permute-start.4 = (bf16[256,256]{0,1:T(8,128)(2,1)S(1)}, bf16[256,256]{0,1:T(8,128)(2,1)S(1)}, u32[]{:S(2)}, u32[]{:S(2)}) collective-permute-start(bf16[256,256]{0,1:T(8,128)(2,1)S(1)} %collective-permute-done.3), channel_id=1, source_target_pairs={{0,28},{4,0},{8,4},{12,8},{16,12},{20,16},{24,20},{28,24},{1,29},{... | collective-permute-start | bytes 393224 | tf_op jit(solution)/shard_map/ppermute | solution.py:86
  48.0 9.0 %collective-permute-start.5 = (bf16[256,256]{0,1:T(8,128)(2,1)S(1)}, bf16[256,256]{0,1:T(8,128)(2,1)S(1)}, u32[]{:S(2)}, u32[]{:S(2)}) collective-permute-start(bf16[256,256]{0,1:T(8,128)(2,1)S(1)} %collective-permute-done.4), channel_id=1, source_target_pairs={{0,28},{4,0},{8,4},{12,8},{16,12},{20,16},{24,20},{28,24},{1,29},{... | collective-permute-start | bytes 393224 | tf_op jit(solution)/shard_map/ppermute | solution.py:86
  57.0 7.7 %collective-permute-start.6 = (bf16[256,256]{0,1:T(8,128)(2,1)S(1)}, bf16[256,256]{0,1:T(8,128)(2,1)S(1)}, u32[]{:S(2)}, u32[]{:S(2)}) collective-permute-start(bf16[256,256]{0,1:T(8,128)(2,1)S(1)} %collective-permute-done.5), channel_id=1, source_target_pairs={{0,28},{4,0},{8,4},{12,8},{16,12},{20,16},{24,20},{28,24},{1,29},{... | collective-permute-start | bytes 393224 | tf_op jit(solution)/shard_map/ppermute | solution.py:86
  66.0 63.4 %reduce-scatter.2.cloned.1.call-start = ((), (), s32[]{:S(2)}) async-start(), calls=%async_computation.1 | async-start | bytes 1310720 | tf_op jit(solution)/shard_map/reduce_scatter | solution.py:102
  66.3 5.8 %copy-start.6 = (f32[256,256]{1,0:T(8,128)S(1)}, f32[256,256]{1,0:T(8,128)}, u32[]{:S(2)}) copy-start(f32[256,256]{1,0:T(8,128)} %param.10) | copy-start | bytes 786436
  130.5 2.4 collective-permute-start.7
  198.8 19.6 %collective-permute-start.8 = (f32[768,256]{0,1:T(8,128)S(1)}, f32[768,256]{0,1:T(8,128)S(1)}, u32[]{:S(2)}, u32[]{:S(2)}) collective-permute-start(f32[768,256]{0,1:T(8,128)S(1)} %pad_maximum_fusion.2), channel_id=1, source_target_pairs={{0,2},{1,3},{2,0},{3,1},{4,6},{5,7},{6,4},{7,5},{8,10},{9,11},{10,... | collective-permute-start | bytes 2359304 | tf_op jit(solution)/shard_map/ppermute | solution.py:15
  284.3 18.9 %collective-permute-start.9 = (f32[768,256]{0,1:T(8,128)S(1)}, f32[768,256]{0,1:T(8,128)}, u32[]{:S(2)}, u32[]{:S(2)}) collective-permute-start(f32[768,256]{0,1:T(8,128)S(1)} %pad_maximum_fusion.3), channel_id=1, source_target_pairs={{0,4},{4,0},{8,12},{12,8},{16,20},{20,16},{24,28},{28,24},{1,5},{5... | collective-permute-start | bytes 2359304 | tf_op jit(solution)/shard_map/ppermute | solution.py:15
  372.4 18.0 %collective-permute-start.10 = (f32[768,256]{0,1:T(8,128)S(1)}, f32[768,256]{0,1:T(8,128)}, u32[]{:S(2)}, u32[]{:S(2)}) collective-permute-start(f32[768,256]{0,1:T(8,128)S(1)} %pad_maximum_fusion.4), channel_id=1, source_target_pairs={{0,8},{4,12},{8,0},{12,4},{16,24},{20,28},{24,16},{28,20},{1,9},{5... | collective-permute-start | bytes 2359304 | tf_op jit(solution)/shard_map/ppermute | solution.py:15
  398.2 11.8 %copy-start.5 = (f32[256,256]{1,0:T(8,128)}, f32[256,256]{1,0:T(8,128)S(1)}, u32[]{:S(2)}) copy-start(f32[256,256]{1,0:T(8,128)S(1)} %fusion.59) | copy-start | bytes 786436
  434.1 2.7 copy-start.1
  441.9 0.7 copy-start.7
  442.5 0.7 copy-start
  469.3 35.1 %collective-permute-start.11 = (f32[768,256]{0,1:T(8,128)}, f32[768,256]{0,1:T(8,128)}, u32[]{:S(2)}, u32[]{:S(2)}) collective-permute-start(f32[768,256]{0,1:T(8,128)} %pad_maximum_fusion.5), channel_id=1, source_target_pairs={{0,16},{4,20},{8,24},{12,28},{16,0},{20,4},{24,8},{28,12},{1,17},{... | collective-permute-start | bytes 2359304 | tf_op jit(solution)/shard_map/ppermute | solution.py:15
  546.4 25.4 %copy-start.2 = (f32[1,256,256]{2,1,0:T(8,128)S(1)}, f32[1,256,256]{2,1,0:T(8,128)}, u32[]{:S(2)}) copy-start(f32[1,256,256]{2,1,0:T(8,128)} %fusion.42) | copy-start | bytes 786436
  546.4 25.4 %copy-start.3 = (f32[1,256,256]{2,1,0:T(8,128)S(1)}, f32[1,256,256]{2,1,0:T(8,128)}, u32[]{:S(2)}) copy-start(f32[1,256,256]{2,1,0:T(8,128)} %fusion.38) | copy-start | bytes 786436
  546.4 25.4 %copy-start.4 = (f32[1,256,256]{2,1,0:T(8,128)S(1)}, f32[1,256,256]{2,1,0:T(8,128)}, u32[]{:S(2)}) copy-start(f32[1,256,256]{2,1,0:T(8,128)} %fusion.34) | copy-start | bytes 786436
Sparse Core Ops, SparseCore 0:
  66.2 35.2 all-reduce.2
  104.6 24.8 reduce-scatter.1
